TPU v7x, 32 devices: a whole 2x2x4 slice. The times are simulated.
32 devices in a mesh: obs: 4 (over z), src: 8 (over y, x, core).
Axes of the slice: x: 2, y: 2, z: 4, core: 2. Of those that a mesh axis runs over, the one named last changes fastest.
Arguments:
- delay_near: bfloat16 [16384, 16384], P('src', 'obs'), may hold values from -0.0625 to 0.0625
- delay_far: bfloat16 [16384, 16384], P('src', 'obs'), may hold values from -0.046875 to 0.046875
- incident: bfloat16 [4, 16384, 192], P(None, 'src'), may hold values from -6 to 6
- current_prev: bfloat16 [16384, 192], P('obs'), may hold values from -0.8984375 to 0.8984375
- current_prev2: bfloat16 [16384, 192], P('obs'), may hold values from -0.8984375 to 0.8984375
Outputs:
- currents: bfloat16 [4, 16384, 192], P(None, 'obs')
All inputs are finite; a program needn't handle non-finite values.
Results may differ from a plain program's by a relative error of at most 0.003.
Values may be sent and summed in bfloat16 or wider, within the bound.
No kernel may reach another device: no remote copies, remote signals or barrier semaphores. Data moves between devices by JAX's collectives and lax.ppermute only.
A program may use at most 128 MiB of HBM per device.

v0:
```python
import jax
import jax.numpy as jnp
from jax import lax
from jax.sharding import PartitionSpec as P

STEPS = 4


def broadcast(block, axis, owner):
    block = jnp.where(lax.axis_index(axis) == owner, block, jnp.zeros_like(block))
    return lax.psum(block, axis)


def per_device(delay_near, delay_far, incident, current_prev, current_prev2):
    lagged = current_prev2
    latest = current_prev
    group_ratio = lax.axis_size("src") // lax.axis_size("obs")
    source_index = lax.axis_index("obs")
    share_rows = delay_near.shape[0] // lax.axis_size("obs")
    history = []
    for moment in range(STEPS):

        def partial_term(first_row, row_count, newer_rows=latest, older_rows=lagged):
            total = jnp.dot(delay_near, newer_rows, preferred_element_type=jnp.float32)
            return total + jnp.dot(delay_far, older_rows, preferred_element_type=jnp.float32)

        field_share = lax.psum_scatter(
            partial_term(jnp.int32(0), share_rows * lax.axis_size("obs")),
            "obs",
            scatter_dimension=0,
            tiled=True,
        )
        local_field = lax.dynamic_slice_in_dim(
            incident[moment], source_index * share_rows, share_rows, 0
        )
        law_piece = jnp.tanh(local_field.astype(jnp.float32) - field_share).astype(jnp.bfloat16)
        block_current = lax.all_gather(law_piece, "obs", axis=0, tiled=True)
        pieces = []
        for member in range(group_ratio):
            root_index = source_index * group_ratio + member
            pieces.append(broadcast(block_current, "src", root_index))
        new_current = jnp.concatenate(pieces, axis=0)
        history.append(new_current)
        lagged = latest
        latest = new_current
    return jnp.stack(history)


def solution(mesh):
    in_specs = (
        P("src", "obs"),
        P("src", "obs"),
        P(None, "src", None),
        P("obs", None),
        P("obs", None),
    )
    out_specs = P(None, "obs", None)
    return jax.shard_map(
        per_device, mesh=mesh, in_specs=in_specs, out_specs=out_specs, check_vma=False
    )
```

profile of v0, /device:TPU:0, one launch (start us, length us, event | category | flops | bytes accessed | tf_op | source)
XLA Modules:
  0.0 559.5 jit_solution(12740833205425219651)
XLA Ops:
  6.5 1.4 copy-done
  7.9 9.4 %fusion.12 = f32[2048,192]{0,1:T(8,128)S(1)} fusion(bf16[2048,4096]{1,0:T(8,128)(2,1)} %param.5, bf16[4096,192]{0,1:T(8,128)(2,1)S(1)} %copy-done), kind=kOutput, calls=%fused_computation.36 | convolution fusion | flops 3221225472 | bytes 19922944 | tf_op jit(solution)/shard_map/dot_general | solution.py:24
  17.3 1.3 copy-done.7
  18.6 6.8 %convolution_add_fusion.2 = f32[2048,192]{0,1:T(8,128)} fusion(f32[2048,192]{0,1:T(8,128)S(1)} %fusion.12, bf16[2048,4096]{1,0:T(8,128)(2,1)S(1)} %copy-done.7, bf16[4096,192]{0,1:T(8,128)(2,1)S(1)} %copy-done.8), kind=kOutput, calls=%fused_computation.7 | convolution fusion | flops 3221618688 | bytes 21495808 | tf_op jit(solution)/shard_map/dot_general | solution.py:25
  25.5 3.4 fusion.11
  28.9 34.9 %reduce-scatter.5.cloned.1.call-done = f32[512,192]{0,1:T(8,128)} async-done(((f32[2048,192]{0,1:T(8,128)}), f32[512,192]{0,1:T(8,128)}) %reduce-scatter.5.cloned.1.call-update) | async-done | bytes 393232 | tf_op jit(solution)/shard_map/reduce_scatter | solution.py:27
  64.8 17.9 %all_gather.12 = bf16[2048,192]{0,1:T(8,128)(2,1)S(1)} all-gather(bf16[512,192]{0,1:T(8,128)(2,1)S(1)} %fusion.10), channel_id=1, replica_groups=mesh['obs'=4,'src'=8] {'obs'}, dimensions={0}, use_global_device_ids=true | all-gather | bytes 983040 | tf_op jit(solution)/shard_map/all_gather | solution.py:37
  82.7 1.3 broadcast_select_fusion.3
  84.0 10.4 %fusion.13 = f32[2048,192]{0,1:T(8,128)} fusion(bf16[2048,4096]{1,0:T(8,128)(2,1)} %param.6, bf16[4096,192]{0,1:T(8,128)(2,1)S(1)} %copy-done), kind=kOutput, calls=%fused_computation.37 | convolution fusion | flops 3221225472 | bytes 19922944 | tf_op jit(solution)/shard_map/dot_general | solution.py:25
  94.4 48.0 %all-reduce.15.cloned.1.call-done = (bf16[2048,192]{0,1:T(8,128)(2,1)}, bf16[2048,192]{0,1:T(8,128)(2,1)}) async-done(((bf16[2048,192]{0,1:T(8,128)(2,1)}, bf16[2048,192]{0,1:T(8,128)(2,1)}), (bf16[2048,192]{0,1:T(8,128)(2,1)}, bf16[2048,192]{0,1:T(8,128)(2,1)})) %all-reduce.15.cloned.1.call-update) | async-done | bytes 1572880 | tf_op jit(solution)/shard_map/psum | solution.py:11
  142.4 1.3 constant_dynamic-update-slice_fusion.1
  143.8 11.0 %fusion = f32[2048,192]{0,1:T(8,128)} fusion(f32[2048,192]{0,1:T(8,128)} %fusion.13, bf16[4096,192]{0,1:T(8,128)(2,1)S(1)} %constant_dynamic-update-slice_fusion, bf16[2048,4096]{1,0:T(8,128)(2,1)} %param.5), kind=kOutput, calls=%fused_computation.2 | convolution fusion | flops 3221618688 | bytes 21495808 | tf_op jit(solution)/shard_map/dot_general | solution.py:24
  154.9 34.8 %reduce-scatter.7.cloned.1.call-done = f32[512,192]{0,1:T(8,128)} async-done(((f32[2048,192]{0,1:T(8,128)}), f32[512,192]{0,1:T(8,128)}) %reduce-scatter.7.cloned.1.call-update) | async-done | bytes 393232 | tf_op jit(solution)/shard_map/reduce_scatter | solution.py:27
  190.7 18.1 %all_gather.13 = bf16[2048,192]{0,1:T(8,128)(2,1)S(1)} all-gather(bf16[512,192]{0,1:T(8,128)(2,1)S(1)} %fusion.8), channel_id=1, replica_groups=mesh['obs'=4,'src'=8] {'obs'}, dimensions={0}, use_global_device_ids=true | all-gather | bytes 983040 | tf_op jit(solution)/shard_map/all_gather | solution.py:37
  208.8 1.3 broadcast_select_fusion.2
  210.2 58.3 %all-reduce.13.cloned.1.call-done = (bf16[2048,192]{0,1:T(8,128)(2,1)}, bf16[2048,192]{0,1:T(8,128)(2,1)}) async-done(((bf16[2048,192]{0,1:T(8,128)(2,1)}, bf16[2048,192]{0,1:T(8,128)(2,1)}), (bf16[2048,192]{0,1:T(8,128)(2,1)}, bf16[2048,192]{0,1:T(8,128)(2,1)})) %all-reduce.13.cloned.1.call-update) | async-done | bytes 1572880 | tf_op jit(solution)/shard_map/psum | solution.py:11
  268.5 1.3 constant_dynamic-update-slice_fusion.3
  270.0 10.9 %fusion.14 = f32[192,2048]{1,0:T(8,128)} fusion(bf16[4096,192]{0,1:T(8,128)(2,1)S(1)} %constant_dynamic-update-slice_fusion.2, bf16[2048,4096]{1,0:T(8,128)(2,1)} %param.5), kind=kOutput, calls=%fused_computation.38 | convolution fusion | flops 3221225472 | bytes 19922944 | tf_op jit(solution)/shard_map/dot_general | solution.py:24
  280.9 11.0 %fusion.2 = f32[2048,192]{0,1:T(8,128)} fusion(f32[192,2048]{1,0:T(8,128)} %fusion.14, bf16[4096,192]{0,1:T(8,128)(2,1)S(1)} %constant_dynamic-update-slice_fusion, bf16[2048,4096]{1,0:T(8,128)(2,1)} %param.6), kind=kOutput, calls=%fused_computation.6 | convolution fusion | flops 3221618688 | bytes 21495808 | tf_op jit(solution)/shard_map/dot_general | solution.py:25
  292.0 34.8 %reduce-scatter.9.cloned.1.call-done = f32[512,192]{0,1:T(8,128)} async-done(((f32[2048,192]{0,1:T(8,128)}), f32[512,192]{0,1:T(8,128)}) %reduce-scatter.9.cloned.1.call-update) | async-done | bytes 393232 | tf_op jit(solution)/shard_map/reduce_scatter | solution.py:27
  327.9 17.9 %all_gather.14 = bf16[2048,192]{0,1:T(8,128)(2,1)S(1)} all-gather(bf16[512,192]{0,1:T(8,128)(2,1)S(1)} %fusion.6), channel_id=1, replica_groups=mesh['obs'=4,'src'=8] {'obs'}, dimensions={0}, use_global_device_ids=true | all-gather | bytes 983040 | tf_op jit(solution)/shard_map/all_gather | solution.py:37
  345.8 1.3 broadcast_select_fusion.1
  347.1 58.3 %all-reduce.11.cloned.1.call-done = (bf16[2048,192]{0,1:T(8,128)(2,1)}, bf16[2048,192]{0,1:T(8,128)(2,1)}) async-done(((bf16[2048,192]{0,1:T(8,128)(2,1)}, bf16[2048,192]{0,1:T(8,128)(2,1)}), (bf16[2048,192]{0,1:T(8,128)(2,1)}, bf16[2048,192]{0,1:T(8,128)(2,1)})) %all-reduce.11.cloned.1.call-update) | async-done | bytes 1572880 | tf_op jit(solution)/shard_map/psum | solution.py:11
  405.4 2.2 constant_dynamic-update-slice_fusion.5
  408.7 13.1 %fusion.15 = f32[192,2048]{1,0:T(8,128)} fusion(bf16[4096,192]{0,1:T(8,128)(2,1)} %constant_dynamic-update-slice_fusion.4, bf16[2048,4096]{1,0:T(8,128)(2,1)} %param.5), kind=kOutput, calls=%fused_computation.39 | convolution fusion | flops 3221225472 | bytes 19922944 | tf_op jit(solution)/shard_map/dot_general | solution.py:24
  421.7 11.0 %fusion.1 = f32[2048,192]{0,1:T(8,128)} fusion(f32[192,2048]{1,0:T(8,128)} %fusion.15, bf16[4096,192]{0,1:T(8,128)(2,1)S(1)} %constant_dynamic-update-slice_fusion.2, bf16[2048,4096]{1,0:T(8,128)(2,1)} %param.6), kind=kOutput, calls=%fused_computation.4 | convolution fusion | flops 3221618688 | bytes 21495808 | tf_op jit(solution)/shard_map/dot_general | solution.py:25
  432.8 34.8 %reduce-scatter.11.cloned.1.call-done = f32[512,192]{0,1:T(8,128)} async-done(((f32[2048,192]{0,1:T(8,128)}), f32[512,192]{0,1:T(8,128)}) %reduce-scatter.11.cloned.1.call-update) | async-done | bytes 393232 | tf_op jit(solution)/shard_map/reduce_scatter | solution.py:27
  468.7 17.9 %all_gather.15 = bf16[2048,192]{0,1:T(8,128)(2,1)S(1)} all-gather(bf16[512,192]{0,1:T(8,128)(2,1)S(1)} %fusion.4), channel_id=1, replica_groups=mesh['obs'=4,'src'=8] {'obs'}, dimensions={0}, use_global_device_ids=true | all-gather | bytes 983040 | tf_op jit(solution)/shard_map/all_gather | solution.py:37
  486.6 1.3 broadcast_select_fusion.4
  487.9 58.5 %all-reduce.9.cloned.1.call-done = (bf16[2048,192]{0,1:T(8,128)(2,1)}, bf16[2048,192]{0,1:T(8,128)(2,1)}) async-done(((bf16[2048,192]{0,1:T(8,128)(2,1)}, bf16[2048,192]{0,1:T(8,128)(2,1)}), (bf16[2048,192]{0,1:T(8,128)(2,1)}, bf16[2048,192]{0,1:T(8,128)(2,1)})) %all-reduce.9.cloned.1.call-update) | async-done | bytes 1572880 | tf_op jit(solution)/shard_map/psum | solution.py:11
  546.4 1.6 maximum_bitcast_fusion
  548.3 4.4 pad_maximum_fusion
  (39 shorter events, 6.5 us)
Async XLA Ops:
  6.5 1.4 copy-start
  6.5 10.8 %copy-start.8 = (bf16[4096,192]{0,1:T(8,128)(2,1)S(1)}, bf16[4096,192]{0,1:T(8,128)(2,1)}, u32[]{:S(2)}) copy-start(bf16[4096,192]{0,1:T(8,128)(2,1)} %param.9) | copy-start | bytes 4718596
  6.5 57.2 %reduce-scatter.5.cloned.1.call-start = ((), (), s32[]{:S(2)}) async-start(), calls=%async_computation.4 | async-start | bytes 1966080 | tf_op jit(solution)/shard_map/reduce_scatter | solution.py:27
  7.9 10.7 %copy-start.7 = (bf16[2048,4096]{1,0:T(8,128)(2,1)S(1)}, bf16[2048,4096]{1,0:T(8,128)(2,1)}, u32[]{:S(2)}) copy-start(bf16[2048,4096]{1,0:T(8,128)(2,1)} %param.6) | copy-start | bytes 50331652
  25.4 116.9 %all-reduce.15.cloned.1.call-start = ((), (), s32[]{:S(2)}) async-start(), calls=%async_computation.11 | async-start | bytes 3145728 | tf_op jit(solution)/shard_map/psum | solution.py:11
  84.0 105.6 %reduce-scatter.7.cloned.1.call-start = ((), (), s32[]{:S(2)}) async-start(), calls=%async_computation.5 | async-start | bytes 1966080 | tf_op jit(solution)/shard_map/reduce_scatter | solution.py:27
  142.4 1.4 copy-start.4
  154.8 113.7 %all-reduce.13.cloned.1.call-start = ((), (), s32[]{:S(2)}) async-start(), calls=%async_computation.10 | async-start | bytes 3145728 | tf_op jit(solution)/shard_map/psum | solution.py:11
  210.1 116.6 %reduce-scatter.9.cloned.1.call-start = ((), (), s32[]{:S(2)}) async-start(), calls=%async_computation.6 | async-start | bytes 1966080 | tf_op jit(solution)/shard_map/reduce_scatter | solution.py:27
  268.5 1.4 copy-start.5
  270.0 151.8 %copy-start.2 = (bf16[4096,192]{0,1:T(8,128)(2,1)}, bf16[4096,192]{0,1:T(8,128)(2,1)S(1)}, u32[]{:S(2)}) copy-start(bf16[4096,192]{0,1:T(8,128)(2,1)S(1)} %constant_dynamic-update-slice_fusion.2) | copy-start | bytes 4718596
  291.9 113.5 %all-reduce.11.cloned.1.call-start = ((), (), s32[]{:S(2)}) async-start(), calls=%async_computation.9 | async-start | bytes 3145728 | tf_op jit(solution)/shard_map/psum | solution.py:11
  347.0 120.5 %reduce-scatter.11.cloned.1.call-start = ((), (), s32[]{:S(2)}) async-start(), calls=%async_computation.7 | async-start | bytes 1966080 | tf_op jit(solution)/shard_map/reduce_scatter | solution.py:27
  405.4 2.2 copy-start.6
  432.8 113.6 %all-reduce.9.cloned.1.call-start = ((), (), s32[]{:S(2)}) async-start(), calls=%async_computation.8 | async-start | bytes 3145728 | tf_op jit(solution)/shard_map/psum | solution.py:11
  546.4 1.9 copy-start.3
  548.2 4.4 copy-start.1
Sparse Core Ops, SparseCore 0:
  25.5 38.1 reduce-scatter.4
  84.1 58.1 all-reduce.14
  155.0 34.6 reduce-scatter.6
  210.3 58.2 all-reduce.12
  292.1 34.6 reduce-scatter.8
  347.2 58.2 all-reduce.10
  432.9 34.6 reduce-scatter.10
  488.0 58.3 all-reduce.8
where the time goes:
time: 560 us
  waiting for transfers between devices  362 us (65%)
  matrix products  83.5 us (15%)
  blocking collectives  71.8 us (13%)
  other arithmetic  15.5 us (3%)
  between operations  13.6 us (2%)
  local copies, waits for them, and re-layouts  12.5 us (2%)
    psum x4, waiting for transfers between devices, broadcast(): return lax.psum(block, axis)  223 us
    reduce_scatter x4, waiting for transfers between devices, per_device(): lax.psum_scatter(partial_term(jnp.int32(0), share_rows * lax.axis_size('o...  139 us
    all_gather x4, blocking collectives, per_device(): block_current = lax.all_gather(law_piece, 'obs', axis=0, tiled=True)  71.8 us
    dot_general x4, matrix products, partial_term(): total = jnp.dot(delay_near, newer_rows, preferred_element_type=jnp.float32)  44.3 us
    dot_general x4, matrix products, partial_term(): jnp.dot(delay_far, older_rows, preferred_element_type=jnp.float32)  39.1 us
  transfers between devices with their start and end apart: 8, of which 8 were waited for; matrix products, arithmetic and copies ran while one was open for 2% of the time, Pallas kernels for 0%

commit v1 on v0

v1 whole, which is shorter than its diff:
```python
import jax
import jax.numpy as jnp
from jax import lax
from jax.experimental import pallas as pl
from jax.experimental.pallas import tpu as pltpu
from jax.sharding import PartitionSpec as P


STEPS = 4
PARTS = 2
GRANT = 6 << 20
STREAM_GRANT = 36 << 20


def each_strip(rows, body):
    tall = min(rows, 512)

    def step(i, carry):
        body(i, pl.ds(pl.multiple_of(i * tall, tall), tall))
        return carry

    lax.fori_loop(0, rows // tall, step, 0)
    return rows // tall


def columns(place, wide):
    return pl.ds(pl.multiple_of(place * wide, wide), wide)


def table_of(places):
    return jnp.stack([jnp.int32(place) for place in places])


def joined(refs, n):
    parts = [jnp.concatenate([ref[...] for ref in refs[k : k + n]], axis=1) for k in range(0, len(refs), n)]
    return jnp.concatenate(parts, axis=0)


def product(left, rhs):
    return lax.dot_general(left, rhs, (((1,), (1,)), ((), ())), preferred_element_type=jnp.float32).T


def streamed_sum(matrix, blocks, places):
    rows, width = matrix.shape
    n = len(places)
    part, wide = blocks[0].shape
    count = part * len(blocks) // n
    tall = min(rows, 512)

    def kernel(table_ref, matrix_ref, *refs):
        rhs = joined(refs[:-1], n)
        left = jnp.concatenate([matrix_ref[:, columns(table_ref[k], wide)] for k in range(n)], axis=1)
        refs[-1][...] = product(left, rhs)

    return pl.pallas_call(
        kernel,
        grid_spec=pltpu.PrefetchScalarGridSpec(
            num_scalar_prefetch=1,
            grid=(rows // tall,),
            in_specs=[pl.BlockSpec((tall, width), lambda i, table: (i, 0))]
            + [pl.BlockSpec(block.shape, lambda i, table: (0, 0)) for block in blocks],
            out_specs=pl.BlockSpec((count, tall), lambda i, table: (0, i)),
        ),
        out_shape=jax.ShapeDtypeStruct((count, rows), jnp.float32),
        cost_estimate=pl.CostEstimate(
            flops=2 * rows * width * count, bytes_accessed=2 * rows * width, transcendentals=0
        ),
        compiler_params=pltpu.CompilerParams(vmem_limit_bytes=STREAM_GRANT),
    )(table_of(places), matrix, *blocks)


def weighted_sum(matrix, blocks, places, start=None):
    rows = matrix.shape[0]
    n = len(places)
    part, wide = blocks[0].shape
    count = part * len(blocks) // n
    total_blocks = len(blocks)

    def kernel(table_ref, matrix_ref, *refs):
        out = refs[-1]
        rhs = joined(refs[:total_blocks], n)

        def add(i, cut):
            left = jnp.concatenate([matrix_ref[cut, columns(table_ref[k], wide)] for k in range(n)], axis=1)
            total = product(left, rhs)
            if start is not None:
                total = total + refs[total_blocks][:, cut]
            out[:, cut] = total

        each_strip(rows, add)

    operands = [table_of(places), matrix, *blocks] + ([] if start is None else [start])
    vmem = pl.BlockSpec(memory_space=pltpu.VMEM)
    return pl.pallas_call(
        kernel,
        in_specs=[pl.BlockSpec(memory_space=pltpu.SMEM)] + [vmem] * (len(operands) - 1),
        out_specs=vmem,
        out_shape=jax.ShapeDtypeStruct((count, rows), jnp.float32),
        cost_estimate=pl.CostEstimate(
            flops=2 * rows * n * wide * count, bytes_accessed=2 * rows * n * wide, transcendentals=0
        ),
        compiler_params=pltpu.CompilerParams(vmem_limit_bytes=GRANT),
    )(*operands)


def record(history, moment, blocks, places, width):
    part, wide = blocks[0].shape
    n = len(blocks)
    count = part * n // len(places)

    def kernel(table_ref, *refs):
        out, sems = refs[-2], refs[-1]
        copies = []
        for k in range(n):
            which, place = divmod(k, len(places))
            spot = out.at[moment, pl.ds(which * part, part), columns(table_ref[place], wide)]
            copies.append(pltpu.make_async_copy(refs[k], spot, sems.at[k]))
        for copy in copies:
            copy.start()
        for copy in copies:
            copy.wait()

    in_specs = [pl.BlockSpec(memory_space=pltpu.SMEM)] + [pl.BlockSpec(memory_space=pltpu.VMEM)] * n
    operands = [table_of(places), *blocks]
    aliases = {}
    if history is not None:
        in_specs.append(pl.BlockSpec(memory_space=pl.ANY))
        operands.append(history)
        aliases = {n + 1: 0}
    return pl.pallas_call(
        kernel,
        in_specs=in_specs,
        out_specs=pl.BlockSpec(memory_space=pl.ANY),
        out_shape=jax.ShapeDtypeStruct((STEPS, count, width), jnp.bfloat16),
        scratch_shapes=[pltpu.SemaphoreType.DMA((n,))],
        input_output_aliases=aliases,
        cost_estimate=pl.CostEstimate(flops=0, bytes_accessed=4 * count * width, transcendentals=0),
        compiler_params=pltpu.CompilerParams(vmem_limit_bytes=GRANT),
    )(*operands)


def per_device(delay_near, delay_far, incident, current_prev, current_prev2):
    no, ns = lax.axis_size("obs"), lax.axis_size("src")
    group = ns // no
    rows, width = delay_near.shape
    piece = rows // no

    scale = 1.0
    while 2 * scale * (width * 0.140625 + 6.0) < 65504.0:
        scale *= 2

    z = lax.axis_index("obs")
    s = lax.axis_index("src")
    chip, core = s // group, s % group

    def swap(value, axis, shift):
        if shift == 0:
            return value
        size = no if axis == "obs" else ns
        return lax.ppermute(value, axis, [(i, i ^ shift) for i in range(size)])

    def exchange(partial):
        got = []
        for r in range(no):
            block = lax.dynamic_slice_in_dim(partial, (chip ^ r) * piece, piece, 1)
            got.append(swap(block, "src", group * r))
        got = jnp.stack(got)
        total = None
        for r in range(no):
            block = lax.dynamic_index_in_dim(got, chip ^ z ^ r, 0, keepdims=False)
            block = swap(block, "obs", r)
            block = block.astype(jnp.float32)
            total = block if total is None else total + block
        return total

    def gather(block):
        blocks, places = [], []
        for r in range(no):
            got = swap(block, "src", group * r)
            for k in range(group):
                blocks.append(swap(got, "src", k))
                places.append((core ^ k) * no + (chip ^ r))
        if piece % 128:
            whole = jnp.zeros((block.shape[0], width), block.dtype)
            for got, place in zip(blocks, places):
                whole = lax.dynamic_update_slice_in_dim(whole, got, place * piece, 1)
            blocks, places = [whole], [0]
        return blocks, places

    field = streamed_sum(delay_far, [current_prev2.T], [0])
    far = pltpu.with_memory_space_constraint(delay_far, pltpu.VMEM)
    near = pltpu.with_memory_space_constraint(delay_near, pltpu.VMEM)
    field = weighted_sum(near, [current_prev.T], [0], field)
    newer = ([current_prev.T], [0])
    history = None
    part = current_prev.shape[1] // PARTS
    for moment in range(STEPS):
        last = moment + 1 == STEPS
        local = incident[moment].T.astype(jnp.float32)
        mine = jnp.where(chip == z, local, jnp.zeros_like(local))
        partial = ((mine - field) * scale).astype(jnp.float16)
        totals = [exchange(partial[k * part : (k + 1) * part]) for k in range(PARTS)]
        if moment:
            history = record(history, moment - 1, *newer, width)
        if not last:
            field = weighted_sum(far, *newer)
        blocks = []
        for total in totals:
            law = jnp.tanh(total * (1.0 / scale)).astype(jnp.bfloat16)
            got, places = gather(law)
            blocks += got
        newer = (blocks, places)
        if not last:
            field = weighted_sum(near, *newer, field)
    history = record(history, STEPS - 1, *newer, width)
    return history.transpose(0, 2, 1)


def solution(mesh):
    in_specs = (
        P("src", "obs"),
        P("src", "obs"),
        P(None, "src", None),
        P("obs", None),
        P("obs", None),
    )
    out_specs = P(None, "obs", None)
    return jax.shard_map(
        per_device, mesh=mesh, in_specs=in_specs, out_specs=out_specs, check_vma=False
    )
```

time: 560 us -> 238 us (0.42)
  waiting for transfers between devices: 362 us -> 43.8 us
  starting transfers between devices: 0.3 us -> 106 us
  matrix products: 83.5 us -> 0 us
  blocking collectives: 71.8 us -> 0 us
  Pallas kernels: 0 us -> 60.4 us
  between operations: 13.6 us -> 0.88 us
  other arithmetic: 15.5 us -> 5.26 us
  local copies, waits for them, and re-layouts: 12.5 us -> 20.8 us
    psum x4 -> x0, waiting for transfers between devices: 223 us -> none  [broadcast(): return lax.psum(block, axis)]
    reduce_scatter x4 -> x0, waiting for transfers between devices: 139 us -> none  [per_device(): lax.psum_scatter(partial_term(jnp.int32(0), share_rows * lax.axis_size('o...]
    ppermute x0 -> x104, starting transfers between devices: none -> 106 us  [swap(): return lax.ppermute(value, axis, [(i, i ^ shift) for i in range(size)])]
    dot_general x8 -> x0, matrix products: 83.5 us -> none  [the longest x4 44.3 us: partial_term(): total = jnp.dot(delay_near, newer_rows, preferred_element_type=jnp.float32)]
    all_gather x4 -> x0, blocking collectives: 71.8 us -> none  [per_device(): block_current = lax.all_gather(law_piece, 'obs', axis=0, tiled=True)]
    pallas_call x0 -> x12, Pallas kernels: none -> 60.4 us  [the longest x7 42.7 us: weighted_sum(): pl.pallas_call(kernel, in_specs=[pl.BlockSpec(memory_space=pltpu.SMEM)] +...]
    ppermute x0 -> x104, waiting for transfers between devices: none -> 43.8 us  [swap(): return lax.ppermute(value, axis, [(i, i ^ shift) for i in range(size)])]
    unnamed x21 -> x40, local copies, waits for them, and re-layouts: 7.92 us -> 19 us
  transfers between devices with their start and end apart: 8 -> 104, of which waited for: 8 -> 24; matrix products, arithmetic and copies ran while one was open for 2% -> 1% of each run, Pallas kernels for 0% -> 10%
where the time goes in v1:
time: 238 us; the launch traced here: 237 us
  starting transfers between devices  106 us (45%)
  Pallas kernels  60.4 us (25%)
  waiting for transfers between devices  43.8 us (18%)
  local copies, waits for them, and re-layouts  20.8 us (9%)
  other arithmetic  5.26 us (2%)
    ppermute x104, starting transfers between devices, swap(): return lax.ppermute(value, axis, [(i, i ^ shift) for i in range(size)])  106 us
    ppermute x104, waiting for transfers between devices, swap(): return lax.ppermute(value, axis, [(i, i ^ shift) for i in range(size)])  43.8 us
    pallas_call x7, Pallas kernels, weighted_sum(): pl.pallas_call(kernel, in_specs=[pl.BlockSpec(memory_space=pltpu.SMEM)] +...  42.7 us
    unnamed x40, local copies, waits for them, and re-layouts  19 us
    pallas_call x1, Pallas kernels, streamed_sum(): pl.pallas_call(kernel, grid_spec=pltpu.PrefetchScalarGridSpec(num_scalar_...  9.61 us
    pallas_call x4, Pallas kernels, record(): pl.pallas_call(kernel, in_specs=in_specs, out_specs=pl.BlockSpec(memory_s...  8 us
  transfers between devices with their start and end apart: 104, of which 24 were waited for; matrix products, arithmetic and copies ran while one was open for 1% of the time, Pallas kernels for 10%

profile of v1, /device:TPU:0, one launch (start us, length us, event | category | flops | bytes accessed | tf_op | source)
XLA Modules:
  0.0 237.1 jit_solution(4369146673031646480)
XLA Ops:
  1.4 9.6 %shard_map.55.refs_1_ = f32[192,2048]{1,0:T(8,128)S(1)} custom-call(s32[1]{0:T(128)} %constant.111.clone.1.table_ref, bf16[2048,4096]{1,0:T(8,128)(2,1)} %matrix_ref.14, bf16[192,4096]{1,0:T(8,128)(2,1)S(1)} %bitcast.159), custom_call_target="tpu_custom_call" | custom-call | flops 3221225472 | bytes 16777216 | tf_op jit(solution)/shard_map/pallas_call | solution.py:55
  12.5 5.5 %shard_map.56 = f32[192,2048]{1,0:T(8,128)S(1)} custom-call(s32[1]{0:T(128)} %constant.111.clone.1.table_ref, bf16[2048,4096]{1,0:T(8,128)(2,1)S(1)} %copy-done.1, bf16[192,4096]{1,0:T(8,128)(2,1)S(1)} %bitcast.157, f32[192,2048]{1,0:T(8,128)S(1)} %shard_map.55.refs_1_), custom_call_target="tpu_custom_call" | custom-call | flops 3221225472 | bytes 16777216 | tf_op jit(solution)/shard_map/pallas_call | solution.py:94
  19.7 3.0 %collective-permute-start.13 = (f16[96,512]{1,0:T(8,128)(2,1)S(1)}, f16[96,512]{1,0:T(8,128)(2,1)S(1)}, u32[]{:S(2)}, u32[]{:S(2)}) collective-permute-start(f16[96,512]{1,0:T(8,128)(2,1)S(1)} %get-tuple-element.61), channel_id=1, source_target_pairs={{0,2},{1,3},{2,0},{3,1},{4,6},{5,7},{6,4},{7,5},{8,10},{9,11},{10,... | collective-permute-start | bytes 294920 | tf_op jit(solution)/shard_map/ppermute | solution.py:160
  32.6 2.6 %collective-permute-start.17 = (f16[96,512]{1,0:T(8,128)(2,1)S(1)}, f16[96,512]{1,0:T(8,128)(2,1)S(1)}, u32[]{:S(2)}, u32[]{:S(2)}) collective-permute-start(f16[96,512]{1,0:T(8,128)(2,1)S(1)} %get-tuple-element.57), channel_id=1, source_target_pairs={{0,16},{8,24},{16,0},{24,8},{1,17},{9,25},{17,1},{25,9},{2,18},{10... | collective-permute-start | bytes 294920 | tf_op jit(solution)/shard_map/ppermute | solution.py:160
  36.3 3.5 %collective-permute-start.4 = (f16[96,512]{1,0:T(8,128)(2,1)S(1)}, f16[96,512]{1,0:T(8,128)(2,1)S(1)}, u32[]{:S(2)}, u32[]{:S(2)}) collective-permute-start(f16[96,512]{1,0:T(8,128)(2,1)S(1)} %get-tuple-element.64), channel_id=1, source_target_pairs={{0,16},{8,24},{16,0},{24,8},{1,17},{9,25},{17,1},{25,9},{2,18},{10... | collective-permute-start | bytes 294920 | tf_op jit(solution)/shard_map/ppermute | solution.py:160
  39.8 2.1 collective-permute-start.5
  43.9 3.0 %collective-permute-start.24 = (bf16[96,512]{1,0:T(8,128)(2,1)S(1)}, bf16[96,512]{1,0:T(8,128)(2,1)}, u32[]{:S(2)}, u32[]{:S(2)}) collective-permute-start(bf16[96,512]{1,0:T(8,128)(2,1)S(1)} %fusion.42.refs_8_), channel_id=1, source_target_pairs={{0,6},{1,7},{2,4},{3,5},{4,2},{5,3},{6,0},{7,1},{8,14},{9,15},{10,... | collective-permute-start | bytes 294920 | tf_op jit(solution)/shard_map/ppermute | solution.py:160
  46.9 2.2 collective-permute-done.4
  49.9 2.1 collective-permute-start.11
  53.9 2.8 %collective-permute-done.9.refs_4_ = bf16[96,512]{1,0:T(8,128)(2,1)} collective-permute-done((bf16[96,512]{1,0:T(8,128)(2,1)S(1)}, bf16[96,512]{1,0:T(8,128)(2,1)}, u32[]{:S(2)}, u32[]{:S(2)}) %collective-permute-start.9) | collective-permute-done | bytes 98336 | tf_op jit(solution)/shard_map/ppermute | solution.py:160
  59.7 5.8 %copy-done = bf16[2048,4096]{1,0:T(8,128)(2,1)S(1)} copy-done((bf16[2048,4096]{1,0:T(8,128)(2,1)S(1)}, bf16[2048,4096]{1,0:T(8,128)(2,1)}, u32[]{:S(2)}) %copy-start) | copy-done | bytes 16777240
  65.5 5.5 %shard_map.57.refs_16_ = f32[192,2048]{1,0:T(8,128)S(1)} custom-call(s32[1]{0:T(128)} %constant.111.clone.1.table_ref, bf16[2048,4096]{1,0:T(8,128)(2,1)S(1)} %copy-done, bf16[192,4096]{1,0:T(8,128)(2,1)S(1)} %bitcast.158), custom_call_target="tpu_custom_call" | custom-call | flops 3221225472 | bytes 16777216 | tf_op jit(solution)/shard_map/pallas_call | solution.py:94
  71.1 5.8 %copy-done.2 = bf16[2048,4096]{1,0:T(8,128)(2,1)S(1)} copy-done((bf16[2048,4096]{1,0:T(8,128)(2,1)S(1)}, bf16[2048,4096]{1,0:T(8,128)(2,1)}, u32[]{:S(2)}) %copy-start.2) | copy-done | bytes 16777240
  79.5 6.8 %shard_map.58 = f32[192,2048]{1,0:T(8,128)S(1)} custom-call(s32[8]{0:T(128)S(1)} %stack.106.table_ref, bf16[2048,4096]{1,0:T(8,128)(2,1)S(1)} %copy-done.2, bf16[96,512]{1,0:T(8,128)(2,1)S(1)} %fusion.47.refs_0_, bf16[96,512]{1,0:T(8,128)(2,1)S(1)} %copy-done.10, bf16[96,512]{1,0:T(8,128)(2,1)} %collective-permute-done.7.refs_2_, ...), custom_call_target="tpu_custom_call" | custom-call | flops 3221225472 | bytes 16777216 | tf_op jit(solution)/shard_map/pallas_call | solution.py:94
  95.4 2.1 collective-permute-done.40
  97.7 2.2 collective-permute-start.42
  104.0 2.4 %collective-permute-start.30 = (f16[96,512]{1,0:T(8,128)(2,1)S(1)}, f16[96,512]{1,0:T(8,128)(2,1)S(1)}, u32[]{:S(2)}, u32[]{:S(2)}) collective-permute-start(f16[96,512]{1,0:T(8,128)(2,1)S(1)} %get-tuple-element.50), channel_id=1, source_target_pairs={{0,16},{8,24},{16,0},{24,8},{1,17},{9,25},{17,1},{25,9},{2,18},{10... | collective-permute-start | bytes 294920 | tf_op jit(solution)/shard_map/ppermute | solution.py:160
  109.3 3.1 %collective-permute-start.46 = (bf16[96,512]{1,0:T(8,128)(2,1)S(1)}, bf16[96,512]{1,0:T(8,128)(2,1)S(1)}, u32[]{:S(2)}, u32[]{:S(2)}) collective-permute-start(bf16[96,512]{1,0:T(8,128)(2,1)S(1)} %fusion.32.refs_8_), channel_id=1, source_target_pairs={{0,2},{1,3},{2,0},{3,1},{4,6},{5,7},{6,4},{7,5},{8,10},{9,11},{10,... | collective-permute-start | bytes 294920 | tf_op jit(solution)/shard_map/ppermute | solution.py:160
  114.0 3.1 %collective-permute-done.30 = f16[96,512]{1,0:T(8,128)(2,1)S(1)} collective-permute-done((f16[96,512]{1,0:T(8,128)(2,1)S(1)}, f16[96,512]{1,0:T(8,128)(2,1)S(1)}, u32[]{:S(2)}, u32[]{:S(2)}) %collective-permute-start.30) | collective-permute-done | bytes 98336 | tf_op jit(solution)/shard_map/ppermute | solution.py:160
  122.4 2.3 collective-permute-done.35.refs_4_
  126.4 7.0 %shard_map.59.refs_16_ = f32[192,2048]{1,0:T(8,128)S(1)} custom-call(s32[8]{0:T(128)S(1)} %stack.106.table_ref, bf16[2048,4096]{1,0:T(8,128)(2,1)S(1)} %bitcast.156, bf16[96,512]{1,0:T(8,128)(2,1)S(1)} %fusion.47.refs_0_, bf16[96,512]{1,0:T(8,128)(2,1)S(1)} %copy-done.10, bf16[96,512]{1,0:T(8,128)(2,1)} %collective-permute-done.7.refs_2_, ...), custom_call_target="tpu_custom_call" | custom-call | flops 3221225472 | bytes 16777216 | tf_op jit(solution)/shard_map/pallas_call | solution.py:94
  133.5 6.0 %shard_map.60 = f32[192,2048]{1,0:T(8,128)S(1)} custom-call(s32[8]{0:T(128)S(1)} %stack.106.table_ref, bf16[2048,4096]{1,0:T(8,128)(2,1)S(1)} %copy-done.3, bf16[96,512]{1,0:T(8,128)(2,1)S(1)} %fusion.37.refs_0_, bf16[96,512]{1,0:T(8,128)(2,1)S(1)} %collective-permute-done.32.refs_1_, bf16[96,512]{1,0:T(8,128)(2,1)S(1)} %collective-permute-done.33.refs_2_, ...), custom_call_target="tpu_custom_call" | custom-call | flops 3221225472 | bytes 16777216 | tf_op jit(solution)/shard_map/pallas_call | solution.py:94
  149.3 3.0 %collective-permute-start.68 = (f16[96,512]{1,0:T(8,128)(2,1)S(1)}, f16[96,512]{1,0:T(8,128)(2,1)S(1)}, u32[]{:S(2)}, u32[]{:S(2)}) collective-permute-start(f16[96,512]{1,0:T(8,128)(2,1)S(1)} %get-tuple-element.27), channel_id=1, source_target_pairs={{0,8},{8,0},{16,24},{24,16},{1,9},{9,1},{17,25},{25,17},{2,10},{10... | collective-permute-start | bytes 294920 | tf_op jit(solution)/shard_map/ppermute | solution.py:160
  159.4 3.7 %collective-permute-done.69 = f16[96,512]{1,0:T(8,128)(2,1)S(1)} collective-permute-done((f16[96,512]{1,0:T(8,128)(2,1)S(1)}, f16[96,512]{1,0:T(8,128)(2,1)S(1)}, u32[]{:S(2)}, u32[]{:S(2)}) %collective-permute-start.69) | collective-permute-done | bytes 98336 | tf_op jit(solution)/shard_map/ppermute | solution.py:160
  163.2 3.7 %collective-permute-start.72 = (bf16[96,512]{1,0:T(8,128)(2,1)S(1)}, bf16[96,512]{1,0:T(8,128)(2,1)S(1)}, u32[]{:S(2)}, u32[]{:S(2)}) collective-permute-start(bf16[96,512]{1,0:T(8,128)(2,1)S(1)} %fusion.22.refs_8_), channel_id=1, source_target_pairs={{0,2},{1,3},{2,0},{3,1},{4,6},{5,7},{6,4},{7,5},{8,10},{9,11},{10,... | collective-permute-start | bytes 294920 | tf_op jit(solution)/shard_map/ppermute | solution.py:160
  178.6 6.0 %shard_map.61.refs_16_ = f32[192,2048]{1,0:T(8,128)S(1)} custom-call(s32[8]{0:T(128)S(1)} %stack.106.table_ref, bf16[2048,4096]{1,0:T(8,128)(2,1)S(1)} %bitcast.156, bf16[96,512]{1,0:T(8,128)(2,1)S(1)} %fusion.37.refs_0_, bf16[96,512]{1,0:T(8,128)(2,1)S(1)} %collective-permute-done.32.refs_1_, bf16[96,512]{1,0:T(8,128)(2,1)S(1)} %collective-permute-done.33.refs_2_, ...), custom_call_target="tpu_custom_call" | custom-call | flops 3221225472 | bytes 16777216 | tf_op jit(solution)/shard_map/pallas_call | solution.py:94
  184.6 6.0 %shard_map.62 = f32[192,2048]{1,0:T(8,128)S(1)} custom-call(s32[8]{0:T(128)S(1)} %stack.106.table_ref, bf16[2048,4096]{1,0:T(8,128)(2,1)S(1)} %copy-done.3, bf16[96,512]{1,0:T(8,128)(2,1)S(1)} %fusion.27.refs_0_, bf16[96,512]{1,0:T(8,128)(2,1)S(1)} %collective-permute-done.58.refs_1_, bf16[96,512]{1,0:T(8,128)(2,1)S(1)} %collective-permute-done.59.refs_2_, ...), custom_call_target="tpu_custom_call" | custom-call | flops 3221225472 | bytes 16777216 | tf_op jit(solution)/shard_map/pallas_call | solution.py:94
  200.4 2.1 collective-permute-start.94
  209.6 3.2 %collective-permute-done.95 = f16[96,512]{1,0:T(8,128)(2,1)S(1)} collective-permute-done((f16[96,512]{1,0:T(8,128)(2,1)S(1)}, f16[96,512]{1,0:T(8,128)(2,1)S(1)}, u32[]{:S(2)}, u32[]{:S(2)}) %collective-permute-start.95) | collective-permute-done | bytes 98336 | tf_op jit(solution)/shard_map/ppermute | solution.py:160
  216.5 3.2 %collective-permute-done.82 = f16[96,512]{1,0:T(8,128)(2,1)S(1)} collective-permute-done((f16[96,512]{1,0:T(8,128)(2,1)S(1)}, f16[96,512]{1,0:T(8,128)(2,1)S(1)}, u32[]{:S(2)}, u32[]{:S(2)}) %collective-permute-start.82) | collective-permute-done | bytes 98336 | tf_op jit(solution)/shard_map/ppermute | solution.py:160
  225.2 2.6 %collective-permute-done.87.refs_4_ = bf16[96,512]{1,0:T(8,128)(2,1)S(1)} collective-permute-done((bf16[96,512]{1,0:T(8,128)(2,1)S(1)}, bf16[96,512]{1,0:T(8,128)(2,1)S(1)}, u32[]{:S(2)}, u32[]{:S(2)}) %collective-permute-start.87) | collective-permute-done | bytes 98336 | tf_op jit(solution)/shard_map/ppermute | solution.py:160
  228.9 2.5 %shard_map.63.refs_16_ = bf16[4,192,4096]{2,1,0:T(8,128)(2,1)} custom-call(s32[8]{0:T(128)S(1)} %stack.106.table_ref, bf16[96,512]{1,0:T(8,128)(2,1)S(1)} %fusion.47.refs_0_, bf16[96,512]{1,0:T(8,128)(2,1)S(1)} %copy-done.11, bf16[96,512]{1,0:T(8,128)(2,1)} %collective-permute-done.7.refs_2_, bf16[96,512]{1,0:T(8,128)(2,1)} %collective-permute-done.8.refs_3_, ...), custom_call_target="tpu_custom_call" | custom-call | bytes 3145728 | tf_op jit(solution)/shard_map/pallas_call | solution.py:130
  (270 shorter events, 111.7 us)
Async XLA Ops:
  24.3 10.8 %collective-permute-start = (f16[96,512]{1,0:T(8,128)(2,1)S(1)}, f16[96,512]{1,0:T(8,128)(2,1)S(1)}, u32[]{:S(2)}, u32[]{:S(2)}) collective-permute-start(f16[96,512]{1,0:T(8,128)(2,1)S(1)} %get-tuple-element.68), channel_id=1, source_target_pairs={{0,2},{1,3},{2,0},{3,1},{4,6},{5,7},{6,4},{7,5},{8,10},{9,11},{10,... | collective-permute-start | bytes 294920 | tf_op jit(solution)/shard_map/ppermute | solution.py:160
  26.4 9.0 %collective-permute-start.1 = (f16[96,512]{1,0:T(8,128)(2,1)S(1)}, f16[96,512]{1,0:T(8,128)(2,1)S(1)}, u32[]{:S(2)}, u32[]{:S(2)}) collective-permute-start(f16[96,512]{1,0:T(8,128)(2,1)S(1)} %get-tuple-element.67), channel_id=1, source_target_pairs={{0,4},{1,5},{2,6},{3,7},{4,0},{5,1},{6,2},{7,3},{8,12},{9,13},{10,... | collective-permute-start | bytes 294920 | tf_op jit(solution)/shard_map/ppermute | solution.py:160
  30.9 8.9 %collective-permute-start.16 = (f16[96,512]{1,0:T(8,128)(2,1)S(1)}, f16[96,512]{1,0:T(8,128)(2,1)S(1)}, u32[]{:S(2)}, u32[]{:S(2)}) collective-permute-start(f16[96,512]{1,0:T(8,128)(2,1)S(1)} %get-tuple-element.55), channel_id=1, source_target_pairs={{0,8},{8,0},{16,24},{24,16},{1,9},{9,1},{17,25},{25,17},{2,10},{10... | collective-permute-start | bytes 294920 | tf_op jit(solution)/shard_map/ppermute | solution.py:160
  32.6 10.7 %collective-permute-start.17 = (f16[96,512]{1,0:T(8,128)(2,1)S(1)}, f16[96,512]{1,0:T(8,128)(2,1)S(1)}, u32[]{:S(2)}, u32[]{:S(2)}) collective-permute-start(f16[96,512]{1,0:T(8,128)(2,1)S(1)} %get-tuple-element.57), channel_id=1, source_target_pairs={{0,16},{8,24},{16,0},{24,8},{1,17},{9,25},{17,1},{25,9},{2,18},{10... | collective-permute-start | bytes 294920 | tf_op jit(solution)/shard_map/ppermute | solution.py:160
  36.3 12.8 %collective-permute-start.4 = (f16[96,512]{1,0:T(8,128)(2,1)S(1)}, f16[96,512]{1,0:T(8,128)(2,1)S(1)}, u32[]{:S(2)}, u32[]{:S(2)}) collective-permute-start(f16[96,512]{1,0:T(8,128)(2,1)S(1)} %get-tuple-element.64), channel_id=1, source_target_pairs={{0,16},{8,24},{16,0},{24,8},{1,17},{9,25},{17,1},{25,9},{2,18},{10... | collective-permute-start | bytes 294920 | tf_op jit(solution)/shard_map/ppermute | solution.py:160
  39.8 9.3 %collective-permute-start.5 = (f16[96,512]{1,0:T(8,128)(2,1)S(1)}, f16[96,512]{1,0:T(8,128)(2,1)S(1)}, u32[]{:S(2)}, u32[]{:S(2)}) collective-permute-start(f16[96,512]{1,0:T(8,128)(2,1)S(1)} %get-tuple-element.63), channel_id=1, source_target_pairs={{0,24},{8,16},{16,8},{24,0},{1,25},{9,17},{17,9},{25,1},{2,26},{10... | collective-permute-start | bytes 294920 | tf_op jit(solution)/shard_map/ppermute | solution.py:160
  56.7 14.4 %collective-permute-start.23 = (bf16[96,512]{1,0:T(8,128)(2,1)S(1)}, bf16[96,512]{1,0:T(8,128)(2,1)}, u32[]{:S(2)}, u32[]{:S(2)}) collective-permute-start(bf16[96,512]{1,0:T(8,128)(2,1)S(1)} %collective-permute-done.22.refs_12_), channel_id=1, source_target_pairs={{0,1},{1,0},{2,3},{3,2},{4,5},{5,4},{6,7},{7,6},{8,9},{9,8},{10,11... | collective-permute-start | bytes 294920 | tf_op jit(solution)/shard_map/ppermute | solution.py:160
  56.7 14.4 %collective-permute-start.25 = (bf16[96,512]{1,0:T(8,128)(2,1)}, bf16[96,512]{1,0:T(8,128)(2,1)}, u32[]{:S(2)}, u32[]{:S(2)}) collective-permute-start(bf16[96,512]{1,0:T(8,128)(2,1)} %collective-permute-done.24.refs_14_), channel_id=1, source_target_pairs={{0,1},{1,0},{2,3},{3,2},{4,5},{5,4},{6,7},{7,6},{8,9},{9,8},{10,11... | collective-permute-start | bytes 294920 | tf_op jit(solution)/shard_map/ppermute | solution.py:160
  57.9 13.2 %collective-permute-start.10 = (bf16[96,512]{1,0:T(8,128)(2,1)}, bf16[96,512]{1,0:T(8,128)(2,1)}, u32[]{:S(2)}, u32[]{:S(2)}) collective-permute-start(bf16[96,512]{1,0:T(8,128)(2,1)} %collective-permute-done.9.refs_4_), channel_id=1, source_target_pairs={{0,1},{1,0},{2,3},{3,2},{4,5},{5,4},{6,7},{7,6},{8,9},{9,8},{10,11... | collective-permute-start | bytes 294920 | tf_op jit(solution)/shard_map/ppermute | solution.py:160
  58.5 12.5 %collective-permute-start.12 = (bf16[96,512]{1,0:T(8,128)(2,1)}, bf16[96,512]{1,0:T(8,128)(2,1)}, u32[]{:S(2)}, u32[]{:S(2)}) collective-permute-start(bf16[96,512]{1,0:T(8,128)(2,1)} %collective-permute-done.11.refs_6_), channel_id=1, source_target_pairs={{0,1},{1,0},{2,3},{3,2},{4,5},{5,4},{6,7},{7,6},{8,9},{9,8},{10,11... | collective-permute-start | bytes 294920 | tf_op jit(solution)/shard_map/ppermute | solution.py:160
  59.7 11.4 %collective-permute-start.8 = (bf16[96,512]{1,0:T(8,128)(2,1)}, bf16[96,512]{1,0:T(8,128)(2,1)}, u32[]{:S(2)}, u32[]{:S(2)}) collective-permute-start(bf16[96,512]{1,0:T(8,128)(2,1)} %collective-permute-done.7.refs_2_), channel_id=1, source_target_pairs={{0,1},{1,0},{2,3},{3,2},{4,5},{5,4},{6,7},{7,6},{8,9},{9,8},{10,11... | collective-permute-start | bytes 294920 | tf_op jit(solution)/shard_map/ppermute | solution.py:160
  91.9 9.9 %collective-permute-start.26 = (f16[96,512]{1,0:T(8,128)(2,1)S(1)}, f16[96,512]{1,0:T(8,128)(2,1)S(1)}, u32[]{:S(2)}, u32[]{:S(2)}) collective-permute-start(f16[96,512]{1,0:T(8,128)(2,1)S(1)} %get-tuple-element.54), channel_id=1, source_target_pairs={{0,2},{1,3},{2,0},{3,1},{4,6},{5,7},{6,4},{7,5},{8,10},{9,11},{10,... | collective-permute-start | bytes 294920 | tf_op jit(solution)/shard_map/ppermute | solution.py:160
  93.2 9.9 %collective-permute-start.27 = (f16[96,512]{1,0:T(8,128)(2,1)S(1)}, f16[96,512]{1,0:T(8,128)(2,1)S(1)}, u32[]{:S(2)}, u32[]{:S(2)}) collective-permute-start(f16[96,512]{1,0:T(8,128)(2,1)S(1)} %get-tuple-element.53), channel_id=1, source_target_pairs={{0,4},{1,5},{2,6},{3,7},{4,0},{5,1},{6,2},{7,3},{8,12},{9,13},{10,... | collective-permute-start | bytes 294920 | tf_op jit(solution)/shard_map/ppermute | solution.py:160
  93.8 9.3 %collective-permute-start.28 = (f16[96,512]{1,0:T(8,128)(2,1)S(1)}, f16[96,512]{1,0:T(8,128)(2,1)S(1)}, u32[]{:S(2)}, u32[]{:S(2)}) collective-permute-start(f16[96,512]{1,0:T(8,128)(2,1)S(1)} %get-tuple-element.52), channel_id=1, source_target_pairs={{0,6},{1,7},{2,4},{3,5},{4,2},{5,3},{6,0},{7,1},{8,14},{9,15},{10,... | collective-permute-start | bytes 294920 | tf_op jit(solution)/shard_map/ppermute | solution.py:160
  103.3 9.9 %collective-permute-start.29 = (f16[96,512]{1,0:T(8,128)(2,1)S(1)}, f16[96,512]{1,0:T(8,128)(2,1)S(1)}, u32[]{:S(2)}, u32[]{:S(2)}) collective-permute-start(f16[96,512]{1,0:T(8,128)(2,1)S(1)} %get-tuple-element.48), channel_id=1, source_target_pairs={{0,8},{8,0},{16,24},{24,16},{1,9},{9,1},{17,25},{25,17},{2,10},{10... | collective-permute-start | bytes 294920 | tf_op jit(solution)/shard_map/ppermute | solution.py:160
  104.0 13.1 %collective-permute-start.30 = (f16[96,512]{1,0:T(8,128)(2,1)S(1)}, f16[96,512]{1,0:T(8,128)(2,1)S(1)}, u32[]{:S(2)}, u32[]{:S(2)}) collective-permute-start(f16[96,512]{1,0:T(8,128)(2,1)S(1)} %get-tuple-element.50), channel_id=1, source_target_pairs={{0,16},{8,24},{16,0},{24,8},{1,17},{9,25},{17,1},{25,9},{2,18},{10... | collective-permute-start | bytes 294920 | tf_op jit(solution)/shard_map/ppermute | solution.py:160
  106.4 10.7 %collective-permute-start.31 = (f16[96,512]{1,0:T(8,128)(2,1)S(1)}, f16[96,512]{1,0:T(8,128)(2,1)S(1)}, u32[]{:S(2)}, u32[]{:S(2)}) collective-permute-start(f16[96,512]{1,0:T(8,128)(2,1)S(1)} %get-tuple-element.49), channel_id=1, source_target_pairs={{0,24},{8,16},{16,8},{24,0},{1,25},{9,17},{17,9},{25,1},{2,26},{10... | collective-permute-start | bytes 294920 | tf_op jit(solution)/shard_map/ppermute | solution.py:160
  109.3 9.5 %collective-permute-start.46 = (bf16[96,512]{1,0:T(8,128)(2,1)S(1)}, bf16[96,512]{1,0:T(8,128)(2,1)S(1)}, u32[]{:S(2)}, u32[]{:S(2)}) collective-permute-start(bf16[96,512]{1,0:T(8,128)(2,1)S(1)} %fusion.32.refs_8_), channel_id=1, source_target_pairs={{0,2},{1,3},{2,0},{3,1},{4,6},{5,7},{6,4},{7,5},{8,10},{9,11},{10,... | collective-permute-start | bytes 294920 | tf_op jit(solution)/shard_map/ppermute | solution.py:160
  122.4 11.0 %collective-permute-start.49 = (bf16[96,512]{1,0:T(8,128)(2,1)S(1)}, bf16[96,512]{1,0:T(8,128)(2,1)S(1)}, u32[]{:S(2)}, u32[]{:S(2)}) collective-permute-start(bf16[96,512]{1,0:T(8,128)(2,1)S(1)} %collective-permute-done.48.refs_12_), channel_id=1, source_target_pairs={{0,1},{1,0},{2,3},{3,2},{4,5},{5,4},{6,7},{7,6},{8,9},{9,8},{10,11... | collective-permute-start | bytes 294920 | tf_op jit(solution)/shard_map/ppermute | solution.py:160
  143.7 9.2 %collective-permute-start.52 = (f16[96,512]{1,0:T(8,128)(2,1)S(1)}, f16[96,512]{1,0:T(8,128)(2,1)S(1)}, u32[]{:S(2)}, u32[]{:S(2)}) collective-permute-start(f16[96,512]{1,0:T(8,128)(2,1)S(1)} %get-tuple-element.40), channel_id=1, source_target_pairs={{0,2},{1,3},{2,0},{3,1},{4,6},{5,7},{6,4},{7,5},{8,10},{9,11},{10,... | collective-permute-start | bytes 294920 | tf_op jit(solution)/shard_map/ppermute | solution.py:160
  144.9 9.9 %collective-permute-start.53 = (f16[96,512]{1,0:T(8,128)(2,1)S(1)}, f16[96,512]{1,0:T(8,128)(2,1)S(1)}, u32[]{:S(2)}, u32[]{:S(2)}) collective-permute-start(f16[96,512]{1,0:T(8,128)(2,1)S(1)} %get-tuple-element.39), channel_id=1, source_target_pairs={{0,4},{1,5},{2,6},{3,7},{4,0},{5,1},{6,2},{7,3},{8,12},{9,13},{10,... | collective-permute-start | bytes 294920 | tf_op jit(solution)/shard_map/ppermute | solution.py:160
  152.3 10.8 %collective-permute-start.69 = (f16[96,512]{1,0:T(8,128)(2,1)S(1)}, f16[96,512]{1,0:T(8,128)(2,1)S(1)}, u32[]{:S(2)}, u32[]{:S(2)}) collective-permute-start(f16[96,512]{1,0:T(8,128)(2,1)S(1)} %get-tuple-element.29), channel_id=1, source_target_pairs={{0,16},{8,24},{16,0},{24,8},{1,17},{9,25},{17,1},{25,9},{2,18},{10... | collective-permute-start | bytes 294920 | tf_op jit(solution)/shard_map/ppermute | solution.py:160
  152.9 10.2 %collective-permute-start.70 = (f16[96,512]{1,0:T(8,128)(2,1)S(1)}, f16[96,512]{1,0:T(8,128)(2,1)S(1)}, u32[]{:S(2)}, u32[]{:S(2)}) collective-permute-start(f16[96,512]{1,0:T(8,128)(2,1)S(1)} %get-tuple-element.28), channel_id=1, source_target_pairs={{0,24},{8,16},{16,8},{24,0},{1,25},{9,17},{17,9},{25,1},{2,26},{10... | collective-permute-start | bytes 294920 | tf_op jit(solution)/shard_map/ppermute | solution.py:160
  155.0 11.9 %collective-permute-start.55 = (f16[96,512]{1,0:T(8,128)(2,1)S(1)}, f16[96,512]{1,0:T(8,128)(2,1)S(1)}, u32[]{:S(2)}, u32[]{:S(2)}) collective-permute-start(f16[96,512]{1,0:T(8,128)(2,1)S(1)} %get-tuple-element.34), channel_id=1, source_target_pairs={{0,8},{8,0},{16,24},{24,16},{1,9},{9,1},{17,25},{25,17},{2,10},{10... | collective-permute-start | bytes 294920 | tf_op jit(solution)/shard_map/ppermute | solution.py:160
  156.1 13.8 %collective-permute-start.56 = (f16[96,512]{1,0:T(8,128)(2,1)S(1)}, f16[96,512]{1,0:T(8,128)(2,1)S(1)}, u32[]{:S(2)}, u32[]{:S(2)}) collective-permute-start(f16[96,512]{1,0:T(8,128)(2,1)S(1)} %get-tuple-element.36), channel_id=1, source_target_pairs={{0,16},{8,24},{16,0},{24,8},{1,17},{9,25},{17,1},{25,9},{2,18},{10... | collective-permute-start | bytes 294920 | tf_op jit(solution)/shard_map/ppermute | solution.py:160
  157.6 12.4 %collective-permute-start.57 = (f16[96,512]{1,0:T(8,128)(2,1)S(1)}, f16[96,512]{1,0:T(8,128)(2,1)S(1)}, u32[]{:S(2)}, u32[]{:S(2)}) collective-permute-start(f16[96,512]{1,0:T(8,128)(2,1)S(1)} %get-tuple-element.35), channel_id=1, source_target_pairs={{0,24},{8,16},{16,8},{24,0},{1,25},{9,17},{17,9},{25,1},{2,26},{10... | collective-permute-start | bytes 294920 | tf_op jit(solution)/shard_map/ppermute | solution.py:160
  202.5 10.3 %collective-permute-start.95 = (f16[96,512]{1,0:T(8,128)(2,1)S(1)}, f16[96,512]{1,0:T(8,128)(2,1)S(1)}, u32[]{:S(2)}, u32[]{:S(2)}) collective-permute-start(f16[96,512]{1,0:T(8,128)(2,1)S(1)} %get-tuple-element.15), channel_id=1, source_target_pairs={{0,16},{8,24},{16,0},{24,8},{1,17},{9,25},{17,1},{25,9},{2,18},{10... | collective-permute-start | bytes 294920 | tf_op jit(solution)/shard_map/ppermute | solution.py:160
  203.3 9.6 %collective-permute-start.96 = (f16[96,512]{1,0:T(8,128)(2,1)S(1)}, f16[96,512]{1,0:T(8,128)(2,1)S(1)}, u32[]{:S(2)}, u32[]{:S(2)}) collective-permute-start(f16[96,512]{1,0:T(8,128)(2,1)S(1)} %get-tuple-element.14), channel_id=1, source_target_pairs={{0,24},{8,16},{16,8},{24,0},{1,25},{9,17},{17,9},{25,1},{2,26},{10... | collective-permute-start | bytes 294920 | tf_op jit(solution)/shard_map/ppermute | solution.py:160
  205.2 10.3 %collective-permute-start.81 = (f16[96,512]{1,0:T(8,128)(2,1)S(1)}, f16[96,512]{1,0:T(8,128)(2,1)S(1)}, u32[]{:S(2)}, u32[]{:S(2)}) collective-permute-start(f16[96,512]{1,0:T(8,128)(2,1)S(1)} %get-tuple-element.20), channel_id=1, source_target_pairs={{0,8},{8,0},{16,24},{24,16},{1,9},{9,1},{17,25},{25,17},{2,10},{10... | collective-permute-start | bytes 294920 | tf_op jit(solution)/shard_map/ppermute | solution.py:160
  206.3 13.4 %collective-permute-start.82 = (f16[96,512]{1,0:T(8,128)(2,1)S(1)}, f16[96,512]{1,0:T(8,128)(2,1)S(1)}, u32[]{:S(2)}, u32[]{:S(2)}) collective-permute-start(f16[96,512]{1,0:T(8,128)(2,1)S(1)} %get-tuple-element.22), channel_id=1, source_target_pairs={{0,16},{8,24},{16,0},{24,8},{1,17},{9,25},{17,1},{25,9},{2,18},{10... | collective-permute-start | bytes 294920 | tf_op jit(solution)/shard_map/ppermute | solution.py:160
  208.0 11.7 %collective-permute-start.83 = (f16[96,512]{1,0:T(8,128)(2,1)S(1)}, f16[96,512]{1,0:T(8,128)(2,1)S(1)}, u32[]{:S(2)}, u32[]{:S(2)}) collective-permute-start(f16[96,512]{1,0:T(8,128)(2,1)S(1)} %get-tuple-element.21), channel_id=1, source_target_pairs={{0,24},{8,16},{16,8},{24,0},{1,25},{9,17},{17,9},{25,1},{2,26},{10... | collective-permute-start | bytes 294920 | tf_op jit(solution)/shard_map/ppermute | solution.py:160
  225.2 9.9 %collective-permute-start.103 = (bf16[96,512]{1,0:T(8,128)(2,1)S(1)}, bf16[96,512]{1,0:T(8,128)(2,1)S(1)}, u32[]{:S(2)}, u32[]{:S(2)}) collective-permute-start(bf16[96,512]{1,0:T(8,128)(2,1)S(1)} %collective-permute-done.102.refs_14_), channel_id=1, source_target_pairs={{0,1},{1,0},{2,3},{3,2},{4,5},{5,4},{6,7},{7,6},{8,9},{9,8},{10,11... | collective-permute-start | bytes 294920 | tf_op jit(solution)/shard_map/ppermute | solution.py:160
  (92 other events, 803.3 us)
